TPU v7x, 32 devices: a whole 2x2x4 slice. The times are simulated.
32 devices in a mesh: seq: 8 (over y, x, core), dp: 4 (over z).
Axes of the slice: x: 2, y: 2, z: 4, core: 2. Of those that a mesh axis runs over, the one named last changes fastest.
Arguments:
- query: bfloat16 [4, 1536, 1280], P('dp', 'seq'), may hold values from -52 to 52, as said below
- keys: bfloat16 [4, 1536, 1280], P('dp', 'seq'), may hold values from -6 to 6, as said below
- values: bfloat16 [4, 1536, 1280], P('dp', 'seq'), may hold values from -6 to 6
- attn: bfloat16 [4, 1536, 1280], P('dp', 'seq'), may hold values from -6 to 6
- d_block: bfloat16 [4, 1536, 1280], P('dp', 'seq'), may hold values from -6 to 6
- w_out: bfloat16 [1280, 1280], P('dp'), may hold values from -0.15625 to 0.15625
Outputs:
- d_query: bfloat16 [4, 1536, 1280], P('dp', 'seq')
- d_keys: bfloat16 [4, 1536, 1280], P('dp', 'seq')
- d_values: bfloat16 [4, 1536, 1280], P('dp', 'seq')
- d_weight: float32 [1280, 1280], P('dp')
Inputs may be any that keep to these rules, and one draw needn't show every extreme that they name: Some query patches may lie along the sum of two keys of the same video. keys has entries of order one.
All inputs are finite; a program needn't handle non-finite values.
Results may differ from a plain program's by a relative error of at most 0.0058.
Values may be sent and summed in bfloat16 or wider, within the bound.
A program may use at most 64 MiB of HBM per device.

v0:
```python
import jax
import jax.numpy as jnp
from jax import lax
from jax.sharding import PartitionSpec as P

HEAD_DIM = 80


def head_backward(query_h, keys_h, values_h, dout_h, delta_h):
    patch_total = query_h.shape[0]
    block_rows = min(512, patch_total)
    while patch_total % block_rows != 0:
        block_rows = block_rows // 2
    block_total = patch_total // block_rows
    score_scale = HEAD_DIM ** (-0.5)
    contract_last = (((1,), (1,)), ((), ()))
    contract_first = (((0,), (0,)), ((), ()))

    def one_block(carry, inputs):
        keys_grad, values_grad = carry
        query_block, dout_block, delta_block = inputs
        scores = (
            lax.dot_general(query_block, keys_h, contract_last, preferred_element_type=jnp.float32)
            * score_scale
        )
        row_max = jnp.max(scores, axis=1, keepdims=True)
        lse = row_max + jnp.log(jnp.sum(jnp.exp(scores - row_max), axis=1, keepdims=True))
        probs = jnp.exp(scores - lse)
        probs_low = probs.astype(jnp.bfloat16)
        values_grad = values_grad + lax.dot_general(
            probs_low, dout_block, contract_first, preferred_element_type=jnp.float32
        )
        d_probs = lax.dot_general(
            dout_block, values_h, contract_last, preferred_element_type=jnp.float32
        )
        d_scores = (score_scale * probs * (d_probs - delta_block[:, None])).astype(jnp.bfloat16)
        query_grad = jnp.dot(d_scores, keys_h, preferred_element_type=jnp.float32)
        keys_grad = keys_grad + lax.dot_general(
            d_scores, query_block, contract_first, preferred_element_type=jnp.float32
        )
        return ((keys_grad, values_grad), query_grad.astype(jnp.bfloat16))

    empty = jnp.zeros((patch_total, HEAD_DIM), jnp.float32)
    blocked = (
        query_h.reshape(block_total, block_rows, HEAD_DIM),
        dout_h.reshape(block_total, block_rows, HEAD_DIM),
        delta_h.reshape(block_total, block_rows),
    )
    (keys_grad, values_grad), query_blocks = lax.scan(one_block, (empty, empty), blocked)
    return (
        query_blocks.reshape(patch_total, HEAD_DIM),
        keys_grad.astype(jnp.bfloat16),
        values_grad.astype(jnp.bfloat16),
    )


def body(query, keys, values, attn, d_block, w_out):
    seq_count = lax.axis_size("seq")
    dp_count = lax.axis_size("dp")
    tok_rows = query.shape[1]
    features = query.shape[2]
    head_here = features // HEAD_DIM // seq_count
    grad_y = d_block.reshape(tok_rows, features)
    attn_rows = attn.reshape(tok_rows, features)
    d_out = lax.dot_general(
        grad_y,
        lax.all_gather(w_out, "dp", axis=0, tiled=True),
        (((1,), (1,)), ((), ())),
        preferred_element_type=jnp.float32,
    ).astype(jnp.bfloat16)

    def split_heads(array):
        return array.reshape(tok_rows, seq_count, head_here, HEAD_DIM)

    query_all, keys_all, values_all, dout_all, output_all = (
        lax.all_to_all(split_heads(query), "seq", split_axis=1, concat_axis=0, tiled=True),
        lax.all_to_all(split_heads(keys), "seq", split_axis=1, concat_axis=0, tiled=True),
        lax.all_to_all(split_heads(values), "seq", split_axis=1, concat_axis=0, tiled=True),
        lax.all_to_all(split_heads(d_out), "seq", split_axis=1, concat_axis=0, tiled=True),
        lax.all_to_all(split_heads(attn_rows), "seq", split_axis=1, concat_axis=0, tiled=True),
    )
    row_terms = jnp.sum(dout_all.astype(jnp.float32) * output_all.astype(jnp.float32), axis=3)
    query_list = []
    keys_list = []
    values_list = []
    for head in range(head_here):
        gradient = head_backward(
            query_all[:, 0, head],
            keys_all[:, 0, head],
            values_all[:, 0, head],
            dout_all[:, 0, head],
            row_terms[:, 0, head],
        )
        query_list.append(gradient[0])
        keys_list.append(gradient[1])
        values_list.append(gradient[2])
    query_heads = jnp.stack(query_list, axis=1)[:, None]
    keys_heads = jnp.stack(keys_list, axis=1)[:, None]
    values_heads = jnp.stack(values_list, axis=1)[:, None]
    query_back, keys_back, values_back = (
        lax.all_to_all(query_heads, "seq", split_axis=0, concat_axis=1, tiled=True),
        lax.all_to_all(keys_heads, "seq", split_axis=0, concat_axis=1, tiled=True),
        lax.all_to_all(values_heads, "seq", split_axis=0, concat_axis=1, tiled=True),
    )
    factor = 1.0 / float(dp_count * tok_rows * seq_count) ** 0.5
    contract_first = (((0,), (0,)), ((), ()))
    partial_rows = lax.psum_scatter(
        lax.dot_general(attn_rows, grad_y, contract_first, preferred_element_type=jnp.float32)
        * factor,
        "dp",
        scatter_dimension=0,
        tiled=True,
    )
    d_weight = lax.psum(partial_rows, "seq")
    shape_out = (1, tok_rows, features)
    return (
        query_back.reshape(shape_out),
        keys_back.reshape(shape_out),
        values_back.reshape(shape_out),
        d_weight,
    )


def solution(mesh):
    return jax.shard_map(
        body,
        mesh=mesh,
        in_specs=(
            P("dp", "seq", None),
            P("dp", "seq", None),
            P("dp", "seq", None),
            P("dp", "seq", None),
            P("dp", "seq", None),
            P("dp", None),
        ),
        out_specs=(P("dp", "seq", None), P("dp", "seq", None), P("dp", "seq", None), P("dp", None)),
        check_vma=False,
    )
```

profile of v0, /device:TPU:0, one launch (start us, length us, event | category | flops | bytes accessed | tf_op | source)
XLA Modules:
  0.0 278.9 jit_solution(8899856098852248446)
XLA Ops:
  7.9 2.1 copy.112
  10.0 5.2 %all-to-all-start = ((bf16[192,8,2,80]{0,3,2,1:T(8,128)(2,1)}), bf16[192,8,2,80]{0,3,2,1:T(8,128)(2,1)S(1)}, u32[]{:S(2)}, u32[]{:S(2)}) async-start(bf16[192,8,2,80]{0,3,2,1:T(8,128)(2,1)} %bitcast), calls=%async_computation | async-start | bytes 1310720 | tf_op jit(solution)/shard_map/all_to_all | solution.py:76
  15.3 3.8 %convolution_multiply_fusion.2 = f32[1280,1280]{1,0:T(8,128)} fusion(bf16[1,192,1280]{2,1,0:T(8,128)(2,1)S(1)} %copy-done.8, bf16[1,192,1280]{2,1,0:T(8,128)(2,1)S(1)} %copy-done), kind=kOutput, calls=%fused_computation.54 | convolution fusion | flops 630784000 | bytes 7536640 | tf_op jit(solution)/shard_map/dot_general | solution.py:108
  20.2 2.1 copy.114
  22.3 2.1 copy.118
  24.5 1.9 all-to-all-done
  26.3 4.2 %all-to-all-start.1 = ((bf16[192,8,2,80]{0,3,2,1:T(8,128)(2,1)}), bf16[192,8,2,80]{0,3,2,1:T(8,128)(2,1)}, u32[]{:S(2)}, u32[]{:S(2)}) async-start(bf16[192,8,2,80]{0,3,2,1:T(8,128)(2,1)} %bitcast.192), calls=%async_computation.1 | async-start | bytes 1310720 | tf_op jit(solution)/shard_map/all_to_all | solution.py:77
  34.5 7.2 %all-to-all-done.1 = bf16[192,8,2,80]{0,3,2,1:T(8,128)(2,1)} async-done(((bf16[192,8,2,80]{0,3,2,1:T(8,128)(2,1)}), bf16[192,8,2,80]{0,3,2,1:T(8,128)(2,1)}, u32[]{:S(2)}, u32[]{:S(2)}) %all-to-all-start.1) | async-done | bytes 491552 | tf_op jit(solution)/shard_map/all_to_all | solution.py:77
  41.7 4.2 %all-to-all-start.3 = ((bf16[192,8,2,80]{0,3,2,1:T(8,128)(2,1)}), bf16[192,8,2,80]{0,3,2,1:T(8,128)(2,1)}, u32[]{:S(2)}, u32[]{:S(2)}) async-start(bf16[192,8,2,80]{0,3,2,1:T(8,128)(2,1)} %bitcast.13), calls=%async_computation.3 | async-start | bytes 1310720 | tf_op jit(solution)/shard_map/all_to_all | solution.py:78
  48.7 1.8 slice_bitcast_fusion.3
  50.7 6.4 %all-to-all-done.3 = bf16[192,8,2,80]{0,3,2,1:T(8,128)(2,1)} async-done(((bf16[192,8,2,80]{0,3,2,1:T(8,128)(2,1)}), bf16[192,8,2,80]{0,3,2,1:T(8,128)(2,1)}, u32[]{:S(2)}, u32[]{:S(2)}) %all-to-all-start.3) | async-done | bytes 491552 | tf_op jit(solution)/shard_map/all_to_all | solution.py:78
  57.0 2.3 copy.119
  59.3 2.4 all_to_all.107
  61.7 16.2 %all-gather.2.cloned.1.call-done = bf16[1280,1280]{1,0:T(8,128)(2,1)} async-done(((bf16[320,1280]{1,0:T(8,128)(2,1)}), bf16[1280,1280]{1,0:T(8,128)(2,1)}) %all-gather.2.cloned.1.call-update) | async-done | bytes 3276816 | tf_op jit(solution)/shard_map/all_gather | solution.py:67
  77.9 3.9 %convolution_convert_fusion.2 = bf16[192,1280]{1,0:T(8,128)(2,1)} fusion(bf16[1280,1280]{1,0:T(8,128)(2,1)} %all-gather.2.cloned.1.call-done, bf16[1,192,1280]{2,1,0:T(8,128)(2,1)S(1)} %copy-done), kind=kOutput, calls=%fused_computation.55 | convolution fusion | flops 629391360 | bytes 4259840 | tf_op jit(solution)/shard_map/dot_general | solution.py:65
  81.9 2.1 copy.116
  84.0 4.2 %all-to-all-start.2 = ((bf16[192,8,2,80]{0,3,2,1:T(8,128)(2,1)}), bf16[192,8,2,80]{0,3,2,1:T(8,128)(2,1)}, u32[]{:S(2)}, u32[]{:S(2)}) async-start(bf16[192,8,2,80]{0,3,2,1:T(8,128)(2,1)} %bitcast.193), calls=%async_computation.2 | async-start | bytes 1310720 | tf_op jit(solution)/shard_map/all_to_all | solution.py:79
  88.2 1.8 slice_bitcast_fusion.2
  93.0 1.9 copy.130
  94.9 4.5 %all-to-all-done.2 = bf16[192,8,2,80]{0,3,2,1:T(8,128)(2,1)} async-done(((bf16[192,8,2,80]{0,3,2,1:T(8,128)(2,1)}), bf16[192,8,2,80]{0,3,2,1:T(8,128)(2,1)}, u32[]{:S(2)}, u32[]{:S(2)}) %all-to-all-start.2) | async-done | bytes 491552 | tf_op jit(solution)/shard_map/all_to_all | solution.py:79
  99.3 4.4 %all-to-all-start.4 = ((bf16[192,8,2,80]{0,3,2,1:T(8,128)(2,1)}), bf16[192,8,2,80]{0,3,2,1:T(8,128)(2,1)}, u32[]{:S(2)}, u32[]{:S(2)}) async-start(bf16[192,8,2,80]{0,3,2,1:T(8,128)(2,1)} %bitcast.190), calls=%async_computation.4 | async-start | bytes 1310720 | tf_op jit(solution)/shard_map/all_to_all | solution.py:80
  103.7 2.3 copy.117
  106.0 2.4 all_to_all.103
  108.4 1.8 fusion.45
  110.2 1.9 copy.143
  112.1 2.6 all-to-all-done.4
  117.4 31.8 %while.30 = (s32[]{:T(128)}, f32[1536,80]{0,1:T(8,128)S(1)}, f32[1536,80]{0,1:T(8,128)S(1)}, bf16[3,512,80]{1,2,0:T(8,128)(2,1)S(1)}, bf16[3,512,80]{2,1,0:T(8,1...) while((s32[]{:T(128)}, f32[1536,80]{0,1:T(8,128)S(1)}, ...), condition=%wide.region_4.5_spmd.clone, body=%wide.region_1.4_spmd.clone.sunk | while | flops 638328320 | bytes 46932176 | solution.py:49
  121.3 2.8 %convolution_add_fusion.9 = f32[1536,80]{0,1:T(8,128)S(1)} fusion(f32[512,1536]{1,0:T(8,128)} %copy-done.1, f32[512]{0:T(512)S(1)} %log_add_fusion.4, f32[1536,80]{0,1:T(8,128)S(1)} %get-tuple-element.496, pred[]{:T(512)S(6)} %compare.6, bf16[3,512,80]{2,1,0:T(8,128)(2,1)} %get-tuple-element.511, s32[]{:T(128)} %get-tuple-element.494), kind=kOutput, calls=%fused_computation.7.clone.1 | convolution fusion | flops 127647744 | bytes 4262401 | tf_op jit(solution)/shard_map/while/body/eval_jaxpr/dot_general | solution.py:30
  131.9 2.8 %convolution_add_fusion.9 = f32[1536,80]{0,1:T(8,128)S(1)} fusion(f32[512,1536]{1,0:T(8,128)} %copy-done.1, f32[512]{0:T(512)S(1)} %log_add_fusion.4, f32[1536,80]{0,1:T(8,128)S(1)} %get-tuple-element.496, pred[]{:T(512)S(6)} %compare.6, bf16[3,512,80]{2,1,0:T(8,128)(2,1)} %get-tuple-element.511, s32[]{:T(128)} %get-tuple-element.494), kind=kOutput, calls=%fused_computation.7.clone.1 | convolution fusion | flops 127647744 | bytes 4262401 | tf_op jit(solution)/shard_map/while/body/eval_jaxpr/dot_general | solution.py:30
  142.5 2.8 %convolution_add_fusion.9 = f32[1536,80]{0,1:T(8,128)S(1)} fusion(f32[512,1536]{1,0:T(8,128)} %copy-done.1, f32[512]{0:T(512)S(1)} %log_add_fusion.4, f32[1536,80]{0,1:T(8,128)S(1)} %get-tuple-element.496, pred[]{:T(512)S(6)} %compare.6, bf16[3,512,80]{2,1,0:T(8,128)(2,1)} %get-tuple-element.511, s32[]{:T(128)} %get-tuple-element.494), kind=kOutput, calls=%fused_computation.7.clone.1 | convolution fusion | flops 127647744 | bytes 4262401 | tf_op jit(solution)/shard_map/while/body/eval_jaxpr/dot_general | solution.py:30
  145.4 1.8 fusion.92
  150.0 29.2 %while.31 = (s32[]{:T(128)}, f32[1536,80]{0,1:T(8,128)S(1)}, f32[1536,80]{0,1:T(8,128)S(1)}, bf16[3,512,80]{1,2,0:T(8,128)(2,1)S(1)}, bf16[3,512,80]{2,1,0:T(8,1...) while((s32[]{:T(128)}, f32[1536,80]{0,1:T(8,128)S(1)}, ...), condition=%wide.region_8.9_spmd.clone, body=%wide.region_5.8_spmd.clone.sunk | while | flops 638328320 | bytes 48061684 | solution.py:49
  154.0 2.8 %convolution_add_fusion.11 = f32[1536,80]{0,1:T(8,128)S(1)} fusion(f32[512,1536]{1,0:T(8,128)} %copy-done.3, f32[512]{0:T(512)S(1)} %log_add_fusion.5, f32[1536,80]{0,1:T(8,128)S(1)} %get-tuple-element.463, pred[]{:T(512)S(6)} %compare.7, bf16[3,512,80]{2,1,0:T(8,128)(2,1)S(1)} %copy-done.7, s32[]{:T(128)} %get-tuple-element.461), kind=kOutput, calls=%fused_computation.34.clone.1 | convolution fusion | flops 127647744 | bytes 4261893 | tf_op jit(solution)/shard_map/while/body/eval_jaxpr/dot_general | solution.py:30
  163.8 2.8 %convolution_add_fusion.11 = f32[1536,80]{0,1:T(8,128)S(1)} fusion(f32[512,1536]{1,0:T(8,128)} %copy-done.3, f32[512]{0:T(512)S(1)} %log_add_fusion.5, f32[1536,80]{0,1:T(8,128)S(1)} %get-tuple-element.463, pred[]{:T(512)S(6)} %compare.7, bf16[3,512,80]{2,1,0:T(8,128)(2,1)S(1)} %copy-done.7, s32[]{:T(128)} %get-tuple-element.461), kind=kOutput, calls=%fused_computation.34.clone.1 | convolution fusion | flops 127647744 | bytes 4261893 | tf_op jit(solution)/shard_map/while/body/eval_jaxpr/dot_general | solution.py:30
  173.5 2.8 %convolution_add_fusion.11 = f32[1536,80]{0,1:T(8,128)S(1)} fusion(f32[512,1536]{1,0:T(8,128)} %copy-done.3, f32[512]{0:T(512)S(1)} %log_add_fusion.5, f32[1536,80]{0,1:T(8,128)S(1)} %get-tuple-element.463, pred[]{:T(512)S(6)} %compare.7, bf16[3,512,80]{2,1,0:T(8,128)(2,1)S(1)} %copy-done.7, s32[]{:T(128)} %get-tuple-element.461), kind=kOutput, calls=%fused_computation.34.clone.1 | convolution fusion | flops 127647744 | bytes 4261893 | tf_op jit(solution)/shard_map/while/body/eval_jaxpr/dot_general | solution.py:30
  180.4 1.8 copy.137
  182.1 3.5 %all-to-all-start.7 = ((bf16[1536,1,2,80]{3,2,1,0:T(2,128)(2,1)}), bf16[1536,1,2,80]{3,2,1,0:T(2,128)(2,1)S(1)}, u32[]{:S(2)}, u32[]{:S(2)}) async-start(bf16[1536,1,2,80]{3,2,1,0:T(2,128)(2,1)} %copy.137), calls=%async_computation.7 | async-start | bytes 1572864 | tf_op jit(solution)/shard_map/all_to_all | solution.py:103
  185.8 1.8 copy.135
  187.6 10.6 %all-to-all-done.7 = bf16[1536,1,2,80]{3,2,1,0:T(2,128)(2,1)S(1)} async-done(((bf16[1536,1,2,80]{3,2,1,0:T(2,128)(2,1)}), bf16[1536,1,2,80]{3,2,1,0:T(2,128)(2,1)S(1)}, u32[]{:S(2)}, u32[]{:S(2)}) %all-to-all-start.7) | async-done | bytes 491552 | tf_op jit(solution)/shard_map/all_to_all | solution.py:103
  198.2 3.5 %all-to-all-start.6 = ((bf16[1536,1,2,80]{3,2,1,0:T(2,128)(2,1)}), bf16[1536,1,2,80]{3,2,1,0:T(2,128)(2,1)S(1)}, u32[]{:S(2)}, u32[]{:S(2)}) async-start(bf16[1536,1,2,80]{3,2,1,0:T(2,128)(2,1)} %copy.135), calls=%async_computation.6 | async-start | bytes 1572864 | tf_op jit(solution)/shard_map/all_to_all | solution.py:102
  203.7 1.8 copy.132
  205.5 10.5 %all-to-all-done.6 = bf16[1536,1,2,80]{3,2,1,0:T(2,128)(2,1)S(1)} async-done(((bf16[1536,1,2,80]{3,2,1,0:T(2,128)(2,1)}), bf16[1536,1,2,80]{3,2,1,0:T(2,128)(2,1)S(1)}, u32[]{:S(2)}, u32[]{:S(2)}) %all-to-all-start.6) | async-done | bytes 491552 | tf_op jit(solution)/shard_map/all_to_all | solution.py:102
  215.9 3.6 %all-to-all-start.5 = ((bf16[1536,1,2,80]{3,2,1,0:T(2,128)(2,1)}), bf16[1536,1,2,80]{3,2,1,0:T(2,128)(2,1)S(1)}, u32[]{:S(2)}, u32[]{:S(2)}) async-start(bf16[1536,1,2,80]{3,2,1,0:T(2,128)(2,1)} %copy.132), calls=%async_computation.5 | async-start | bytes 1572864 | tf_op jit(solution)/shard_map/all_to_all | solution.py:101
  219.5 1.9 copy.138
  221.4 2.1 copy.141
  225.7 6.2 %all-to-all-done.5 = bf16[1536,1,2,80]{3,2,1,0:T(2,128)(2,1)S(1)} async-done(((bf16[1536,1,2,80]{3,2,1,0:T(2,128)(2,1)}), bf16[1536,1,2,80]{3,2,1,0:T(2,128)(2,1)S(1)}, u32[]{:S(2)}, u32[]{:S(2)}) %all-to-all-start.5) | async-done | bytes 491552 | tf_op jit(solution)/shard_map/all_to_all | solution.py:101
  233.9 35.8 %all-reduce.2.cloned.1.call-done = f32[320,1280]{1,0:T(8,128)} async-done(((f32[320,1280]{1,0:T(8,128)}), f32[320,1280]{1,0:T(8,128)}) %all-reduce.2.cloned.1.call-update) | async-done | bytes 1638416 | tf_op jit(solution)/shard_map/psum | solution.py:114
  269.7 2.7 copy.174
  (134 shorter events, 64.2 us)
Async XLA Ops:
  7.2 8.1 %copy-start = (bf16[1,192,1280]{2,1,0:T(8,128)(2,1)S(1)}, bf16[1,192,1280]{2,1,0:T(8,128)(2,1)}, u32[]{:S(2)}) copy-start(bf16[1,192,1280]{2,1,0:T(8,128)(2,1)} %param.14) | copy-start | bytes 1474564
  7.2 8.1 %copy-start.8 = (bf16[1,192,1280]{2,1,0:T(8,128)(2,1)S(1)}, bf16[1,192,1280]{2,1,0:T(8,128)(2,1)}, u32[]{:S(2)}) copy-start(bf16[1,192,1280]{2,1,0:T(8,128)(2,1)} %param.13) | copy-start | bytes 1474564
  7.2 70.7 %all-gather.2.cloned.1.call-start = ((), (), s32[]{:S(2)}) async-start(), calls=%async_computation.9 | async-start | bytes 4096000 | tf_op jit(solution)/shard_map/all_gather | solution.py:67
  10.0 16.3 %all-to-all-start = ((bf16[192,8,2,80]{0,3,2,1:T(8,128)(2,1)}), bf16[192,8,2,80]{0,3,2,1:T(8,128)(2,1)S(1)}, u32[]{:S(2)}, u32[]{:S(2)}) async-start(bf16[192,8,2,80]{0,3,2,1:T(8,128)(2,1)} %bitcast), calls=%async_computation | async-start | bytes 1310720 | tf_op jit(solution)/shard_map/all_to_all | solution.py:76
  15.2 186.6 %reduce-scatter.2.cloned.1.call-start = ((), (), s32[]{:S(2)}) async-start(), calls=%async_computation.10 | async-start | bytes 8192000 | tf_op jit(solution)/shard_map/reduce_scatter | solution.py:107
  26.3 15.3 %all-to-all-start.1 = ((bf16[192,8,2,80]{0,3,2,1:T(8,128)(2,1)}), bf16[192,8,2,80]{0,3,2,1:T(8,128)(2,1)}, u32[]{:S(2)}, u32[]{:S(2)}) async-start(bf16[192,8,2,80]{0,3,2,1:T(8,128)(2,1)} %bitcast.192), calls=%async_computation.1 | async-start | bytes 1310720 | tf_op jit(solution)/shard_map/all_to_all | solution.py:77
  41.7 15.3 %all-to-all-start.3 = ((bf16[192,8,2,80]{0,3,2,1:T(8,128)(2,1)}), bf16[192,8,2,80]{0,3,2,1:T(8,128)(2,1)}, u32[]{:S(2)}, u32[]{:S(2)}) async-start(bf16[192,8,2,80]{0,3,2,1:T(8,128)(2,1)} %bitcast.13), calls=%async_computation.3 | async-start | bytes 1310720 | tf_op jit(solution)/shard_map/all_to_all | solution.py:78
  84.0 15.4 %all-to-all-start.2 = ((bf16[192,8,2,80]{0,3,2,1:T(8,128)(2,1)}), bf16[192,8,2,80]{0,3,2,1:T(8,128)(2,1)}, u32[]{:S(2)}, u32[]{:S(2)}) async-start(bf16[192,8,2,80]{0,3,2,1:T(8,128)(2,1)} %bitcast.193), calls=%async_computation.2 | async-start | bytes 1310720 | tf_op jit(solution)/shard_map/all_to_all | solution.py:79
  99.3 15.3 %all-to-all-start.4 = ((bf16[192,8,2,80]{0,3,2,1:T(8,128)(2,1)}), bf16[192,8,2,80]{0,3,2,1:T(8,128)(2,1)}, u32[]{:S(2)}, u32[]{:S(2)}) async-start(bf16[192,8,2,80]{0,3,2,1:T(8,128)(2,1)} %bitcast.190), calls=%async_computation.4 | async-start | bytes 1310720 | tf_op jit(solution)/shard_map/all_to_all | solution.py:80
  118.9 1.7 copy-start.1
  121.2 2.9 %copy-start.2 = (f32[512,1536]{1,0:T(8,128)S(1)}, f32[512,1536]{1,0:T(8,128)}, u32[]{:S(2)}) copy-start(f32[512,1536]{1,0:T(8,128)} %copy-done.1) | copy-start | bytes 9437188 | tf_op jit(solution)/shard_map/while
  121.2 2.9 %copy-start.6 = (bf16[1536,80]{1,0:T(8,128)(2,1)S(1)}, bf16[1536,80]{1,0:T(8,128)(2,1)}, u32[]{:S(2)}) copy-start(bf16[1536,80]{1,0:T(8,128)(2,1)} %get-tuple-element.512) | copy-start | bytes 737284 | tf_op jit(solution)/shard_map/while
  129.5 1.7 copy-start.1
  131.8 2.9 %copy-start.2 = (f32[512,1536]{1,0:T(8,128)S(1)}, f32[512,1536]{1,0:T(8,128)}, u32[]{:S(2)}) copy-start(f32[512,1536]{1,0:T(8,128)} %copy-done.1) | copy-start | bytes 9437188 | tf_op jit(solution)/shard_map/while
  131.8 2.9 %copy-start.6 = (bf16[1536,80]{1,0:T(8,128)(2,1)S(1)}, bf16[1536,80]{1,0:T(8,128)(2,1)}, u32[]{:S(2)}) copy-start(bf16[1536,80]{1,0:T(8,128)(2,1)} %get-tuple-element.512) | copy-start | bytes 737284 | tf_op jit(solution)/shard_map/while
  140.1 1.7 copy-start.1
  142.4 2.9 %copy-start.2 = (f32[512,1536]{1,0:T(8,128)S(1)}, f32[512,1536]{1,0:T(8,128)}, u32[]{:S(2)}) copy-start(f32[512,1536]{1,0:T(8,128)} %copy-done.1) | copy-start | bytes 9437188 | tf_op jit(solution)/shard_map/while
  142.5 2.9 %copy-start.6 = (bf16[1536,80]{1,0:T(8,128)(2,1)S(1)}, bf16[1536,80]{1,0:T(8,128)(2,1)}, u32[]{:S(2)}) copy-start(bf16[1536,80]{1,0:T(8,128)(2,1)} %get-tuple-element.512) | copy-start | bytes 737284 | tf_op jit(solution)/shard_map/while
  150.0 3.9 %copy-start.7 = (bf16[3,512,80]{2,1,0:T(8,128)(2,1)S(1)}, bf16[3,512,80]{2,1,0:T(8,128)(2,1)}, u32[]{:S(2)}) copy-start(bf16[3,512,80]{2,1,0:T(8,128)(2,1)} %get-tuple-element.478) | copy-start | bytes 737284 | tf_op jit(solution)/shard_map/while
  151.7 1.7 copy-start.3
  153.4 3.5 %copy-start.5 = (bf16[1536,80]{1,0:T(8,128)(2,1)S(1)}, bf16[1536,80]{1,0:T(8,128)(2,1)}, u32[]{:S(2)}) copy-start(bf16[1536,80]{1,0:T(8,128)(2,1)} %get-tuple-element.479) | copy-start | bytes 737284 | tf_op jit(solution)/shard_map/while
  154.0 3.0 %copy-start.4 = (f32[512,1536]{1,0:T(8,128)S(1)}, f32[512,1536]{1,0:T(8,128)}, u32[]{:S(2)}) copy-start(f32[512,1536]{1,0:T(8,128)} %copy-done.3) | copy-start | bytes 9437188 | tf_op jit(solution)/shard_map/while
  159.8 4.0 %copy-start.7 = (bf16[3,512,80]{2,1,0:T(8,128)(2,1)S(1)}, bf16[3,512,80]{2,1,0:T(8,128)(2,1)}, u32[]{:S(2)}) copy-start(bf16[3,512,80]{2,1,0:T(8,128)(2,1)} %get-tuple-element.478) | copy-start | bytes 737284 | tf_op jit(solution)/shard_map/while
  161.4 1.7 copy-start.3
  163.2 3.5 %copy-start.5 = (bf16[1536,80]{1,0:T(8,128)(2,1)S(1)}, bf16[1536,80]{1,0:T(8,128)(2,1)}, u32[]{:S(2)}) copy-start(bf16[1536,80]{1,0:T(8,128)(2,1)} %get-tuple-element.479) | copy-start | bytes 737284 | tf_op jit(solution)/shard_map/while
  163.8 2.9 %copy-start.4 = (f32[512,1536]{1,0:T(8,128)S(1)}, f32[512,1536]{1,0:T(8,128)}, u32[]{:S(2)}) copy-start(f32[512,1536]{1,0:T(8,128)} %copy-done.3) | copy-start | bytes 9437188 | tf_op jit(solution)/shard_map/while
  169.5 3.9 %copy-start.7 = (bf16[3,512,80]{2,1,0:T(8,128)(2,1)S(1)}, bf16[3,512,80]{2,1,0:T(8,128)(2,1)}, u32[]{:S(2)}) copy-start(bf16[3,512,80]{2,1,0:T(8,128)(2,1)} %get-tuple-element.478) | copy-start | bytes 737284 | tf_op jit(solution)/shard_map/while
  171.2 1.7 copy-start.3
  172.9 3.5 %copy-start.5 = (bf16[1536,80]{1,0:T(8,128)(2,1)S(1)}, bf16[1536,80]{1,0:T(8,128)(2,1)}, u32[]{:S(2)}) copy-start(bf16[1536,80]{1,0:T(8,128)(2,1)} %get-tuple-element.479) | copy-start | bytes 737284 | tf_op jit(solution)/shard_map/while
  173.5 2.9 %copy-start.4 = (f32[512,1536]{1,0:T(8,128)S(1)}, f32[512,1536]{1,0:T(8,128)}, u32[]{:S(2)}) copy-start(f32[512,1536]{1,0:T(8,128)} %copy-done.3) | copy-start | bytes 9437188 | tf_op jit(solution)/shard_map/while
  179.2 6.5 %copy-start.9 = (bf16[1536,1,80]{0,2,1:T(8,128)(2,1)S(1)}, bf16[1536,1,80]{0,2,1:T(8,128)(2,1)}, u32[]{:S(2)}) copy-start(bf16[1536,1,80]{0,2,1:T(8,128)(2,1)} %get-tuple-element.331) | copy-start | bytes 737284
  182.1 16.1 %all-to-all-start.7 = ((bf16[1536,1,2,80]{3,2,1,0:T(2,128)(2,1)}), bf16[1536,1,2,80]{3,2,1,0:T(2,128)(2,1)S(1)}, u32[]{:S(2)}, u32[]{:S(2)}) async-start(bf16[1536,1,2,80]{3,2,1,0:T(2,128)(2,1)} %copy.137), calls=%async_computation.7 | async-start | bytes 1572864 | tf_op jit(solution)/shard_map/all_to_all | solution.py:103
  198.2 17.7 %all-to-all-start.6 = ((bf16[1536,1,2,80]{3,2,1,0:T(2,128)(2,1)}), bf16[1536,1,2,80]{3,2,1,0:T(2,128)(2,1)S(1)}, u32[]{:S(2)}, u32[]{:S(2)}) async-start(bf16[1536,1,2,80]{3,2,1,0:T(2,128)(2,1)} %copy.135), calls=%async_computation.6 | async-start | bytes 1572864 | tf_op jit(solution)/shard_map/all_to_all | solution.py:102
  201.8 67.9 %all-reduce.2.cloned.1.call-start = ((), (), s32[]{:S(2)}) async-start(), calls=%async_computation.11 | async-start | bytes 3276800 | tf_op jit(solution)/shard_map/psum | solution.py:114
  215.9 16.1 %all-to-all-start.5 = ((bf16[1536,1,2,80]{3,2,1,0:T(2,128)(2,1)}), bf16[1536,1,2,80]{3,2,1,0:T(2,128)(2,1)S(1)}, u32[]{:S(2)}, u32[]{:S(2)}) async-start(bf16[1536,1,2,80]{3,2,1,0:T(2,128)(2,1)} %copy.132), calls=%async_computation.5 | async-start | bytes 1572864 | tf_op jit(solution)/shard_map/all_to_all | solution.py:101
Sparse Core Ops, SparseCore 0:
  9.6 68.3 all-gather.1
  80.2 113.6 reduce-scatter.1
  205.8 63.8 all-reduce.1
where the time goes:
time: 281 us; the launch traced here: 279 us
  waiting for transfers between devices  103 us (37%)
  local copies, waits for them, and re-layouts  67.1 us (24%)
  matrix products  54.1 us (19%)
  starting transfers between devices  33 us (12%)
  between operations  14 us (5%)
  other arithmetic  7.03 us (3%)
    psum x1, waiting for transfers between devices, body(): d_weight = lax.psum(partial_rows, 'seq')  35.8 us
    unnamed x22, local copies, waits for them, and re-layouts  23.1 us
    dot_general x6, matrix products, one_block(): lax.dot_general(probs_low, dout_block, contract_first, preferred_element_...  16.9 us
    all_gather x1, waiting for transfers between devices, body(): lax.all_gather(w_out, 'dp', axis=0, tiled=True)  16.2 us
    while x42, local copies, waits for them, and re-layouts  10.7 us
    all_to_all x1, waiting for transfers between devices, body(): lax.all_to_all(values_heads, 'seq', split_axis=0, concat_axis=1, tiled=True)  10.6 us
    all_to_all x1, waiting for transfers between devices, body(): lax.all_to_all(keys_heads, 'seq', split_axis=0, concat_axis=1, tiled=True)  10.5 us
    dot_general x6, matrix products, one_block(): lax.dot_general(query_block, keys_h, contract_last, preferred_element_typ...  9.55 us
  transfers between devices with their start and end apart: 11, of which 10 were waited for; matrix products, arithmetic and copies ran while one was open for 38% of the time, Pallas kernels for 0%

commit v1 on v0

--- a/solution.py
+++ b/solution.py
@@ -55,6 +55,11 @@
 
 
 def body(query, keys, values, attn, d_block, w_out):
+
+    def time_the_windows(frame_in, across):
+        item_now = lax.all_gather(frame_in, across)
+        return jnp.sum(item_now, axis=0)
+
     seq_count = lax.axis_size("seq")
     dp_count = lax.axis_size("dp")
     tok_rows = query.shape[1]
@@ -111,7 +116,7 @@
         scatter_dimension=0,
         tiled=True,
     )
-    d_weight = lax.psum(partial_rows, "seq")
+    d_weight = time_the_windows(partial_rows, "seq")
     shape_out = (1, tok_rows, features)
     return (
         query_back.reshape(shape_out),

time: 281 us -> 349 us (1.24)
  waiting for transfers between devices: 103 us -> 195 us
  matrix products: 54.1 us -> 40.4 us
  local copies, waits for them, and re-layouts: 67.1 us -> 54.1 us
  other arithmetic: 7.03 us -> 12.2 us
    reduce_scatter x1, waiting for transfers between devices: 0.02 us -> 117 us  [body(): lax.psum_scatter(lax.dot_general(attn_rows, grad_y, contract_first, prefe...]
    psum x1 -> x0, waiting for transfers between devices: 35.8 us -> none  [body(): d_weight = lax.psum(partial_rows, 'seq')]
    dot_general x6, matrix products: 16.9 us -> 4.72 us  [one_block(): lax.dot_general(probs_low, dout_block, contract_first, preferred_element_...]
    while x42 -> x18, local copies, waits for them, and re-layouts: 10.7 us -> 0.05 us
    all_to_all x1, waiting for transfers between devices: 4.46 us -> 14.5 us  [body(): lax.all_to_all(split_heads(d_out), 'seq', split_axis=1, concat_axis=0, ti...]
    reduce_sum x0 -> x1, other arithmetic: none -> 6.92 us  [time_the_windows(): return jnp.sum(item_now, axis=0)]
    unnamed x22 -> x25, local copies, waits for them, and re-layouts: 23.1 us -> 17.5 us
    all_to_all x1, waiting for transfers between devices: 7.23 us -> 1.8 us  [body(): lax.all_to_all(split_heads(keys), 'seq', split_axis=1, concat_axis=0, til...]
  transfers between devices with their start and end apart: 11 -> 11, of which waited for: 10 -> 10; matrix products, arithmetic and copies ran while one was open for 38% -> 24% of each run, Pallas kernels for 0% -> 0%
where the time goes in v1:
time: 349 us; the launch traced here: 347 us
  waiting for transfers between devices  195 us (56%)
  local copies, waits for them, and re-layouts  54.1 us (16%)
  matrix products  40.4 us (12%)
  starting transfers between devices  31.5 us (9%)
  between operations  14.1 us (4%)
  other arithmetic  12.2 us (3%)
    reduce_scatter x1, waiting for transfers between devices, body(): lax.psum_scatter(lax.dot_general(attn_rows, grad_y, contract_first, prefe...  117 us
    unnamed x25, local copies, waits for them, and re-layouts  17.5 us
    all_gather x1, waiting for transfers between devices, body(): lax.all_gather(w_out, 'dp', axis=0, tiled=True)  16.6 us
    all_to_all x1, waiting for transfers between devices, body(): lax.all_to_all(split_heads(d_out), 'seq', split_axis=1, concat_axis=0, ti...  14.5 us
    all_to_all x1, waiting for transfers between devices, body(): lax.all_to_all(keys_heads, 'seq', split_axis=0, concat_axis=1, tiled=True)  10.7 us
    all_to_all x1, waiting for transfers between devices, body(): lax.all_to_all(query_heads, 'seq', split_axis=0, concat_axis=1, tiled=True)  10.5 us
    dot_general x6, matrix products, one_block(): lax.dot_general(query_block, keys_h, contract_last, preferred_element_typ...  9.76 us
    dot_general x6, matrix products, one_block(): lax.dot_general(d_scores, query_block, contract_first, preferred_element_...  8.25 us
  transfers between devices with their start and end apart: 11, of which 10 were waited for; matrix products, arithmetic and copies ran while one was open for 24% of the time, Pallas kernels for 0%

profile of v1, /device:TPU:0, one launch (start us, length us, event | category | flops | bytes accessed | tf_op | source)
XLA Modules:
  0.0 347.3 jit_solution(13246287749584502255)
XLA Ops:
  8.2 4.8 %convolution_multiply_fusion.2 = f32[1280,1280]{1,0:T(8,128)} fusion(bf16[1,192,1280]{2,1,0:T(8,128)(2,1)} %param.13, bf16[1,192,1280]{2,1,0:T(8,128)(2,1)S(1)} %copy-done), kind=kOutput, calls=%fused_computation.54 | convolution fusion | flops 630784000 | bytes 7536640 | tf_op jit(solution)/shard_map/dot_general | solution.py:113
  13.9 117.1 %reduce-scatter.2.cloned.1.call-done = f32[320,1280]{1,0:T(8,128)} async-done(((f32[1280,1280]{1,0:T(8,128)}), f32[320,1280]{1,0:T(8,128)}) %reduce-scatter.2.cloned.1.call-update) | async-done | bytes 1638416 | tf_op jit(solution)/shard_map/reduce_scatter | solution.py:112
  132.1 4.2 %all-to-all-start = ((bf16[192,8,2,80]{0,3,2,1:T(8,128)(2,1)}), bf16[192,8,2,80]{0,3,2,1:T(8,128)(2,1)}, u32[]{:S(2)}, u32[]{:S(2)}) async-start(bf16[192,8,2,80]{0,3,2,1:T(8,128)(2,1)} %bitcast), calls=%async_computation | async-start | bytes 1310720 | tf_op jit(solution)/shard_map/all_to_all | solution.py:81
  138.5 2.1 copy.118
  140.7 6.7 %all-to-all-done = bf16[192,8,2,80]{0,3,2,1:T(8,128)(2,1)} async-done(((bf16[192,8,2,80]{0,3,2,1:T(8,128)(2,1)}), bf16[192,8,2,80]{0,3,2,1:T(8,128)(2,1)}, u32[]{:S(2)}, u32[]{:S(2)}) %all-to-all-start) | async-done | bytes 491552 | tf_op jit(solution)/shard_map/all_to_all | solution.py:81
  147.4 3.5 %all-to-all-start.1 = ((bf16[192,8,2,80]{0,3,2,1:T(8,128)(2,1)}), bf16[192,8,2,80]{0,3,2,1:T(8,128)(2,1)S(1)}, u32[]{:S(2)}, u32[]{:S(2)}) async-start(bf16[192,8,2,80]{0,3,2,1:T(8,128)(2,1)} %bitcast.194), calls=%async_computation.1 | async-start | bytes 1310720 | tf_op jit(solution)/shard_map/all_to_all | solution.py:82
  151.0 2.3 copy.113
  153.2 2.4 all_to_all.95
  155.6 1.8 fusion.46
  157.4 1.9 copy.142
  160.2 1.8 all-to-all-done.1
  162.0 4.2 %all-to-all-start.3 = ((bf16[192,8,2,80]{0,3,2,1:T(8,128)(2,1)}), bf16[192,8,2,80]{0,3,2,1:T(8,128)(2,1)}, u32[]{:S(2)}, u32[]{:S(2)}) async-start(bf16[192,8,2,80]{0,3,2,1:T(8,128)(2,1)} %bitcast.13), calls=%async_computation.3 | async-start | bytes 1310720 | tf_op jit(solution)/shard_map/all_to_all | solution.py:83
  167.4 1.7 all_to_all.99
  169.7 7.7 %all-to-all-done.3 = bf16[192,8,2,80]{0,3,2,1:T(8,128)(2,1)} async-done(((bf16[192,8,2,80]{0,3,2,1:T(8,128)(2,1)}), bf16[192,8,2,80]{0,3,2,1:T(8,128)(2,1)}, u32[]{:S(2)}, u32[]{:S(2)}) %all-to-all-start.3) | async-done | bytes 491552 | tf_op jit(solution)/shard_map/all_to_all | solution.py:83
  177.3 2.3 copy.119
  179.6 2.4 all_to_all.107
  182.0 16.6 %all-gather.4.cloned.1.call-done = bf16[1280,1280]{1,0:T(8,128)(2,1)} async-done(((bf16[320,1280]{1,0:T(8,128)(2,1)}), bf16[1280,1280]{1,0:T(8,128)(2,1)}) %all-gather.4.cloned.1.call-update) | async-done | bytes 3276816 | tf_op jit(solution)/shard_map/all_gather | solution.py:72
  198.7 3.9 %convolution_convert_fusion.2 = bf16[192,1280]{1,0:T(8,128)(2,1)} fusion(bf16[1280,1280]{1,0:T(8,128)(2,1)} %all-gather.4.cloned.1.call-done, bf16[1,192,1280]{2,1,0:T(8,128)(2,1)S(1)} %copy-done), kind=kOutput, calls=%fused_computation.55 | convolution fusion | flops 629391360 | bytes 4259840 | tf_op jit(solution)/shard_map/dot_general | solution.py:70
  202.6 2.1 copy.116
  204.7 4.2 %all-to-all-start.2 = ((bf16[192,8,2,80]{0,3,2,1:T(8,128)(2,1)}), bf16[192,8,2,80]{0,3,2,1:T(8,128)(2,1)}, u32[]{:S(2)}, u32[]{:S(2)}) async-start(bf16[192,8,2,80]{0,3,2,1:T(8,128)(2,1)} %bitcast.195), calls=%async_computation.2 | async-start | bytes 1310720 | tf_op jit(solution)/shard_map/all_to_all | solution.py:84
  208.9 2.0 slice_bitcast_fusion.2
  213.0 14.5 %all-to-all-done.2 = bf16[192,8,2,80]{0,3,2,1:T(8,128)(2,1)} async-done(((bf16[192,8,2,80]{0,3,2,1:T(8,128)(2,1)}), bf16[192,8,2,80]{0,3,2,1:T(8,128)(2,1)}, u32[]{:S(2)}, u32[]{:S(2)}) %all-to-all-start.2) | async-done | bytes 491552 | tf_op jit(solution)/shard_map/all_to_all | solution.py:84
  227.5 4.4 %all-to-all-start.4 = ((bf16[192,8,2,80]{0,3,2,1:T(8,128)(2,1)}), bf16[192,8,2,80]{0,3,2,1:T(8,128)(2,1)}, u32[]{:S(2)}, u32[]{:S(2)}) async-start(bf16[192,8,2,80]{0,3,2,1:T(8,128)(2,1)} %bitcast.192), calls=%async_computation.4 | async-start | bytes 1310720 | tf_op jit(solution)/shard_map/all_to_all | solution.py:85
  231.9 2.3 copy.117
  234.2 2.4 all_to_all.103
  236.6 1.8 fusion.45
  238.3 1.9 copy.143
  241.1 1.9 all-to-all-done.4
  243.0 1.5 fusion.39
  244.7 17.9 %while.31 = (s32[]{:T(128)}, f32[1536,80]{0,1:T(8,128)S(1)}, f32[1536,80]{0,1:T(8,128)S(1)}, bf16[3,512,80]{1,2,0:T(8,128)(2,1)S(1)}, bf16[3,512,80]{2,1,0:T(8,1...) while((s32[]{:T(128)}, f32[1536,80]{0,1:T(8,128)S(1)}, ...), condition=%wide.region_8.9_spmd.clone, body=%wide.region_5.8_spmd.clone.sunk | while | flops 638328320 | bytes 22894800 | solution.py:49
  244.7 1.7 fusion.103
  250.8 1.6 fusion.103
  256.7 1.6 fusion.103
  263.2 17.8 %while.30 = (s32[]{:T(128)}, f32[1536,80]{0,1:T(8,128)S(1)}, f32[1536,80]{0,1:T(8,128)S(1)}, bf16[3,512,80]{1,2,0:T(8,128)(2,1)S(1)}, bf16[3,512,80]{2,1,0:T(8,1...) while((s32[]{:T(128)}, f32[1536,80]{0,1:T(8,128)S(1)}, ...), condition=%wide.region_4.5_spmd.clone, body=%wide.region_1.4_spmd.clone.sunk | while | flops 638328320 | bytes 21911732 | solution.py:49
  263.2 1.6 fusion.91
  269.2 1.6 fusion.91
  275.1 1.6 fusion.91
  281.6 1.8 copy.132
  283.4 3.5 %all-to-all-start.5 = ((bf16[1536,1,2,80]{3,2,1,0:T(2,128)(2,1)}), bf16[1536,1,2,80]{3,2,1,0:T(2,128)(2,1)S(1)}, u32[]{:S(2)}, u32[]{:S(2)}) async-start(bf16[1536,1,2,80]{3,2,1,0:T(2,128)(2,1)} %copy.132), calls=%async_computation.5 | async-start | bytes 1572864 | tf_op jit(solution)/shard_map/all_to_all | solution.py:106
  287.1 1.8 copy.135
  288.9 10.5 %all-to-all-done.5 = bf16[1536,1,2,80]{3,2,1,0:T(2,128)(2,1)S(1)} async-done(((bf16[1536,1,2,80]{3,2,1,0:T(2,128)(2,1)}), bf16[1536,1,2,80]{3,2,1,0:T(2,128)(2,1)S(1)}, u32[]{:S(2)}, u32[]{:S(2)}) %all-to-all-start.5) | async-done | bytes 491552 | tf_op jit(solution)/shard_map/all_to_all | solution.py:106
  299.5 3.5 %all-to-all-start.6 = ((bf16[1536,1,2,80]{3,2,1,0:T(2,128)(2,1)}), bf16[1536,1,2,80]{3,2,1,0:T(2,128)(2,1)S(1)}, u32[]{:S(2)}, u32[]{:S(2)}) async-start(bf16[1536,1,2,80]{3,2,1,0:T(2,128)(2,1)} %copy.135), calls=%async_computation.6 | async-start | bytes 1572864 | tf_op jit(solution)/shard_map/all_to_all | solution.py:107
  303.1 1.8 copy.137
  304.9 10.7 %all-to-all-done.6 = bf16[1536,1,2,80]{3,2,1,0:T(2,128)(2,1)S(1)} async-done(((bf16[1536,1,2,80]{3,2,1,0:T(2,128)(2,1)}), bf16[1536,1,2,80]{3,2,1,0:T(2,128)(2,1)S(1)}, u32[]{:S(2)}, u32[]{:S(2)}) %all-to-all-start.6) | async-done | bytes 491552 | tf_op jit(solution)/shard_map/all_to_all | solution.py:107
  315.5 3.8 %all-to-all-start.7 = ((bf16[1536,1,2,80]{3,2,1,0:T(2,128)(2,1)}), bf16[1536,1,2,80]{3,2,1,0:T(2,128)(2,1)S(1)}, u32[]{:S(2)}, u32[]{:S(2)}) async-start(bf16[1536,1,2,80]{3,2,1,0:T(2,128)(2,1)} %copy.137), calls=%async_computation.7 | async-start | bytes 1572864 | tf_op jit(solution)/shard_map/all_to_all | solution.py:108
  319.3 1.4 copy.146
  325.2 6.4 %all-to-all-done.7 = bf16[1536,1,2,80]{3,2,1,0:T(2,128)(2,1)S(1)} async-done(((bf16[1536,1,2,80]{3,2,1,0:T(2,128)(2,1)}), bf16[1536,1,2,80]{3,2,1,0:T(2,128)(2,1)S(1)}, u32[]{:S(2)}, u32[]{:S(2)}) %all-to-all-start.7) | async-done | bytes 491552 | tf_op jit(solution)/shard_map/all_to_all | solution.py:108
  333.9 6.9 %reduce_sum.40 = f32[320,1280]{1,0:T(8,128)} reduce(f32[8,320,1280]{2,1,0:T(8,128)} %bitcast.184, f32[]{:T(128)} %constant.39.clone.1), dimensions={0}, to_apply=%region_10.11 | reduce | flops 2867200 | bytes 14745604 | tf_op jit(solution)/shard_map/reduce_sum | solution.py:61
  (114 shorter events, 44.5 us)
Async XLA Ops:
  7.2 1.0 copy-start
  7.2 123.8 %reduce-scatter.2.cloned.1.call-start = ((), (), s32[]{:S(2)}) async-start(), calls=%async_computation.10 | async-start | bytes 8192000 | tf_op jit(solution)/shard_map/reduce_scatter | solution.py:112
  13.0 118.0 %copy-start.6 = (bf16[1,192,1280]{2,1,0:T(8,128)(2,1)S(1)}, bf16[1,192,1280]{2,1,0:T(8,128)(2,1)}, u32[]{:S(2)}) copy-start(bf16[1,192,1280]{2,1,0:T(8,128)(2,1)} %param.10) | copy-start | bytes 1474564
  13.0 123.3 %copy-start.5 = (bf16[1,192,1280]{2,1,0:T(8,128)(2,1)S(1)}, bf16[1,192,1280]{2,1,0:T(8,128)(2,1)}, u32[]{:S(2)}) copy-start(bf16[1,192,1280]{2,1,0:T(8,128)(2,1)} %param.13) | copy-start | bytes 1474564
  13.1 124.4 %copy-start.7 = (bf16[1,192,1280]{2,1,0:T(8,128)(2,1)S(1)}, bf16[1,192,1280]{2,1,0:T(8,128)(2,1)}, u32[]{:S(2)}) copy-start(bf16[1,192,1280]{2,1,0:T(8,128)(2,1)} %param.11) | copy-start | bytes 1474564
  13.1 185.6 %all-gather.4.cloned.1.call-start = ((), (), s32[]{:S(2)}) async-start(), calls=%async_computation.9 | async-start | bytes 4096000 | tf_op jit(solution)/shard_map/all_gather | solution.py:72
  13.8 320.1 %all-gather.6.cloned.1.call-start = ((), (), s32[]{:S(2)}) async-start(), calls=%async_computation.11 | async-start | bytes 14745600 | tf_op jit(solution)/shard_map/all_gather | solution.py:60
  132.1 15.3 %all-to-all-start = ((bf16[192,8,2,80]{0,3,2,1:T(8,128)(2,1)}), bf16[192,8,2,80]{0,3,2,1:T(8,128)(2,1)}, u32[]{:S(2)}, u32[]{:S(2)}) async-start(bf16[192,8,2,80]{0,3,2,1:T(8,128)(2,1)} %bitcast), calls=%async_computation | async-start | bytes 1310720 | tf_op jit(solution)/shard_map/all_to_all | solution.py:81
  147.4 14.6 %all-to-all-start.1 = ((bf16[192,8,2,80]{0,3,2,1:T(8,128)(2,1)}), bf16[192,8,2,80]{0,3,2,1:T(8,128)(2,1)S(1)}, u32[]{:S(2)}, u32[]{:S(2)}) async-start(bf16[192,8,2,80]{0,3,2,1:T(8,128)(2,1)} %bitcast.194), calls=%async_computation.1 | async-start | bytes 1310720 | tf_op jit(solution)/shard_map/all_to_all | solution.py:82
  162.0 15.3 %all-to-all-start.3 = ((bf16[192,8,2,80]{0,3,2,1:T(8,128)(2,1)}), bf16[192,8,2,80]{0,3,2,1:T(8,128)(2,1)}, u32[]{:S(2)}, u32[]{:S(2)}) async-start(bf16[192,8,2,80]{0,3,2,1:T(8,128)(2,1)} %bitcast.13), calls=%async_computation.3 | async-start | bytes 1310720 | tf_op jit(solution)/shard_map/all_to_all | solution.py:83
  204.7 22.8 %all-to-all-start.2 = ((bf16[192,8,2,80]{0,3,2,1:T(8,128)(2,1)}), bf16[192,8,2,80]{0,3,2,1:T(8,128)(2,1)}, u32[]{:S(2)}, u32[]{:S(2)}) async-start(bf16[192,8,2,80]{0,3,2,1:T(8,128)(2,1)} %bitcast.195), calls=%async_computation.2 | async-start | bytes 1310720 | tf_op jit(solution)/shard_map/all_to_all | solution.py:84
  227.5 15.5 %all-to-all-start.4 = ((bf16[192,8,2,80]{0,3,2,1:T(8,128)(2,1)}), bf16[192,8,2,80]{0,3,2,1:T(8,128)(2,1)}, u32[]{:S(2)}, u32[]{:S(2)}) async-start(bf16[192,8,2,80]{0,3,2,1:T(8,128)(2,1)} %bitcast.192), calls=%async_computation.4 | async-start | bytes 1310720 | tf_op jit(solution)/shard_map/all_to_all | solution.py:85
  244.7 2.3 copy-start.4
  246.4 1.4 copy-start.2
  250.7 2.2 copy-start.4
  252.4 1.4 copy-start.2
  256.7 2.2 copy-start.4
  258.3 1.4 copy-start.2
  263.2 2.2 copy-start.3
  269.2 2.2 copy-start.3
  275.1 2.2 copy-start.3
  283.4 16.1 %all-to-all-start.5 = ((bf16[1536,1,2,80]{3,2,1,0:T(2,128)(2,1)}), bf16[1536,1,2,80]{3,2,1,0:T(2,128)(2,1)S(1)}, u32[]{:S(2)}, u32[]{:S(2)}) async-start(bf16[1536,1,2,80]{3,2,1,0:T(2,128)(2,1)} %copy.132), calls=%async_computation.5 | async-start | bytes 1572864 | tf_op jit(solution)/shard_map/all_to_all | solution.py:106
  299.5 16.1 %all-to-all-start.6 = ((bf16[1536,1,2,80]{3,2,1,0:T(2,128)(2,1)}), bf16[1536,1,2,80]{3,2,1,0:T(2,128)(2,1)S(1)}, u32[]{:S(2)}, u32[]{:S(2)}) async-start(bf16[1536,1,2,80]{3,2,1,0:T(2,128)(2,1)} %copy.135), calls=%async_computation.6 | async-start | bytes 1572864 | tf_op jit(solution)/shard_map/all_to_all | solution.py:107
  315.5 16.1 %all-to-all-start.7 = ((bf16[1536,1,2,80]{3,2,1,0:T(2,128)(2,1)}), bf16[1536,1,2,80]{3,2,1,0:T(2,128)(2,1)S(1)}, u32[]{:S(2)}, u32[]{:S(2)}) async-start(bf16[1536,1,2,80]{3,2,1,0:T(2,128)(2,1)} %copy.137), calls=%async_computation.7 | async-start | bytes 1572864 | tf_op jit(solution)/shard_map/all_to_all | solution.py:108
  333.9 6.9 %copy-start.1 = (bf16[1,192,1280]{2,1,0:T(8,128)(2,1)S(1)}, bf16[1,192,1280]{2,1,0:T(8,128)(2,1)}, u32[]{:S(2)}) copy-start(bf16[1,192,1280]{2,1,0:T(8,128)(2,1)} %param.14) | copy-start | bytes 1474564
Sparse Core Ops, SparseCore 0:
  13.2 117.7 reduce-scatter.1
  132.5 66.0 all-gather.3
  200.6 84.2 all-gather.5
